TPU v7x, 32 devices: a whole 2x2x4 slice. The times are simulated.
32 devices in a mesh: section: 16 (over z, y, core), dp: 2 (over x).
Axes of the slice: x: 2, y: 2, z: 4, core: 2. Of those that a mesh axis runs over, the one named last changes fastest.
Arguments:
- activations: bfloat16 [16, 16, 64, 4096], P('section', 'dp'), may hold values from -6 to 6
- out_grads: bfloat16 [16, 16, 64, 4096], P('section', 'dp'), may hold values from -6 to 6
- proj_in: bfloat16 [16, 2, 4096, 128], P('section'), may hold values from -0.09375 to 0.09375
- proj_out: bfloat16 [16, 2, 64, 4096], P('section'), may hold values from -0.09375 to 0.09375
- earlier_gram: float32 [8192, 8192], P('section', 'dp'), may hold values from -4 to 4, as said below
Outputs:
- gram: float32 [8192, 8192], P('section', 'dp')
Inputs may be any that keep to these rules, and one draw needn't show every extreme that they name: earlier_gram is symmetric.
All inputs are finite; a program needn't handle non-finite values.
Results may differ from a plain program's by a relative error of at most 0.0013.
Values sent between devices are 32-bit elements; how exact they have to be, the bound alone decides.
A program may use at most 64 MiB of HBM per device.

v0:
```python
import math
import jax
import jax.numpy as jnp
from jax import lax
from jax.sharding import PartitionSpec as P

PROJ = 2
LEN = 64


def per_device(activations, out_grads, proj_in, proj_out, earlier_gram):
    layer_act = activations[0]
    layer_grad = out_grads[0]
    layer_in = proj_in[0]
    layer_out = proj_out[0]
    low_in = jnp.einsum(
        "etd,pdm->petm", layer_act, layer_in, preferred_element_type=jnp.float32
    ).astype(jnp.bfloat16)
    low_out = jnp.einsum(
        "pkd,etd->pekt", layer_out, layer_grad, preferred_element_type=jnp.float32
    ).astype(jnp.bfloat16)
    partial_terms = jnp.einsum(
        "pekt,petm->ekm", low_out, low_in, preferred_element_type=jnp.float32
    )
    local_count = partial_terms.shape[0]
    partial_terms = partial_terms.reshape(local_count, -1)
    n_layers = lax.axis_size("section")
    n_groups = lax.axis_size("dp")
    total_examples = local_count * n_groups
    scale = 1.0 / math.sqrt(LEN * n_layers * PROJ)
    row_width = earlier_gram.shape[0]
    col_width = earlier_gram.shape[1]
    row_start = lax.axis_index("section") * row_width
    col_start = lax.axis_index("dp") * col_width
    summed = lax.psum(partial_terms, "section") * scale
    features = lax.all_gather(summed, "dp", axis=0, tiled=True)
    row_block = lax.dynamic_slice_in_dim(features, row_start, row_width, 1)
    col_block = lax.dynamic_slice_in_dim(features, col_start, col_width, 1)
    outer = jnp.dot(row_block.T, col_block, precision=lax.Precision.HIGHEST)
    return earlier_gram + outer / total_examples


def solution(mesh):
    return jax.shard_map(
        per_device,
        mesh=mesh,
        in_specs=(
            P("section", "dp", None, None),
            P("section", "dp", None, None),
            P("section", None, None, None),
            P("section", None, None, None),
            P("section", "dp"),
        ),
        out_specs=P("section", "dp"),
        check_vma=False,
    )
```

profile of v0, /device:TPU:0, one launch (start us, length us, event | category | flops | bytes accessed | tf_op | source)
XLA Modules:
  0.0 136.9 jit_solution(12887768697109643629)
XLA Ops:
  6.5 0.0 copy-start
  6.5 0.0 all-reduce.2.cloned.1.call-start
  6.5 4.8 %fusion.13 = bf16[2,8,64,64]{3,2,0,1:T(8,128)(2,1)S(1)} fusion(bf16[1,8,64,4096]{3,2,1,0:T(8,128)(2,1)} %param.6, bf16[1,2,64,4096]{3,2,1,0:T(8,128)(2,1)} %param.8), kind=kOutput, calls=%fused_computation.8 | convolution fusion | flops 536936448 | bytes 5373952 | tf_op jit(solution)/shard_map/pkd,etd->pekt/dot_general | solution.py:19
  11.3 0.0 copy-done
  11.3 3.6 %convolution_bitcast_fusion = f32[1,8,64,128]{3,2,1,0:T(8,128)S(1)} fusion(bf16[2,8,64,64]{3,2,0,1:T(8,128)(2,1)S(1)} %fusion.13, bf16[1,8,64,4096]{3,2,1,0:T(8,128)(2,1)} %param.5, bf16[1,2,4096,128]{3,2,1,0:T(8,128)(2,1)S(1)} %copy-done), kind=kOutput, calls=%fused_computation.9 | convolution fusion | flops 1090650112 | bytes 6684672 | tf_op jit(solution)/shard_map/pekt,petm->ekm/dot_general | solution.py:22
  15.0 0.9 copy.11
  15.8 0.0 all-reduce.2.cloned.1.call-update
  15.9 92.6 %all-reduce.2.cloned.1.call-done = f32[8,8192]{1,0:T(8,128)} async-done(((f32[8,8192]{1,0:T(8,128)}), f32[8,8192]{1,0:T(8,128)}) %all-reduce.2.cloned.1.call-update) | async-done | bytes 262160 | tf_op jit(solution)/shard_map/psum | solution.py:35
  108.5 1.0 broadcast_multiply_fusion
  109.4 9.3 %all_gather.3 = f32[16,8192]{1,0:T(8,128)S(1)} all-gather(f32[8,8192]{1,0:T(8,128)S(1)} %broadcast_multiply_fusion), channel_id=1, replica_groups=mesh['section'=16,'dp'=2] {'dp'}, dimensions={0}, use_global_device_ids=true | all-gather | bytes 786432 | tf_op jit(solution)/shard_map/all_gather | solution.py:36
  118.8 11.3 %multiply_add_fusion = f32[512,4096]{1,0:T(8,128)} fusion(f32[512,4096]{1,0:T(8,128)} %param.9, f32[16,8192]{1,0:T(8,128)S(1)} %all_gather.3, s32[]{:T(128)S(6)} %select_n.7, s32[]{:T(128)S(6)} %select_n.6), kind=kOutput, calls=%fused_computation | convolution fusion | flops 406847488 | bytes 17072136 | tf_op jit(solution)/shard_map/dot_general | solution.py:39
Async XLA Ops:
  6.5 4.8 %copy-start = (bf16[1,2,4096,128]{3,2,1,0:T(8,128)(2,1)S(1)}, bf16[1,2,4096,128]{3,2,1,0:T(8,128)(2,1)}, u32[]{:S(2)}) copy-start(bf16[1,2,4096,128]{3,2,1,0:T(8,128)(2,1)} %param.7) | copy-start | bytes 6291460
  6.5 101.9 %all-reduce.2.cloned.1.call-start = ((), (), s32[]{:S(2)}) async-start(), calls=%async_computation | async-start | bytes 524288 | tf_op jit(solution)/shard_map/psum | solution.py:35
Sparse Core Ops, SparseCore 0:
  16.0 92.4 all-reduce.1
where the time goes:
time: 137 us
  waiting for transfers between devices  92.6 us (68%)
  matrix products  19.8 us (14%)
  between operations  13.4 us (10%)
  blocking collectives  9.31 us (7%)
    psum x1, waiting for transfers between devices, per_device(): summed = lax.psum(partial_terms, 'section') * scale  92.6 us
    dot_general x1, matrix products, per_device(): outer = jnp.dot(row_block.T, col_block, precision=lax.Precision.HIGHEST)  11.3 us
    all_gather x1, blocking collectives, per_device(): features = lax.all_gather(summed, 'dp', axis=0, tiled=True)  9.31 us
    dot_general x1, matrix products, per_device(): jnp.einsum('pkd,etd->pekt', layer_out, layer_grad, preferred_element_type...  4.78 us
    dot_general x1, matrix products, per_device(): jnp.einsum('pekt,petm->ekm', low_out, low_in, preferred_element_type=jnp....  3.63 us
  transfers between devices with their start and end apart: 1, of which 1 were waited for; matrix products, arithmetic and copies ran while one was open for 0% of the time, Pallas kernels for 0%

commit v1 on v0

--- a/solution.py
+++ b/solution.py
@@ -32,7 +32,7 @@
     col_width = earlier_gram.shape[1]
     row_start = lax.axis_index("section") * row_width
     col_start = lax.axis_index("dp") * col_width
-    summed = lax.psum(partial_terms, "section") * scale
+    summed = jnp.sum(lax.all_gather(partial_terms, "section"), axis=0) * scale
     features = lax.all_gather(summed, "dp", axis=0, tiled=True)
     row_block = lax.dynamic_slice_in_dim(features, row_start, row_width, 1)
     col_block = lax.dynamic_slice_in_dim(features, col_start, col_width, 1)

time: 137 us -> 99 us (0.72)
  waiting for transfers between devices: 92.6 us -> 53.3 us
  other arithmetic: 0.97 us -> 2.43 us
    psum x1 -> x0, waiting for transfers between devices: 92.6 us -> none  [per_device(): summed = lax.psum(partial_terms, 'section') * scale]
    all_gather x0 -> x1, waiting for transfers between devices: none -> 53.3 us  [per_device(): summed = jnp.sum(lax.all_gather(partial_terms, 'section'), axis=0) * scale]
    reduce_sum x0 -> x1, other arithmetic: none -> 2.4 us  [per_device(): summed = jnp.sum(lax.all_gather(partial_terms, 'section'), axis=0) * scale]
where the time goes in v1:
time: 99 us; the launch traced here: 98.8 us
  waiting for transfers between devices  53.3 us (54%)
  matrix products  19.8 us (20%)
  between operations  13.4 us (14%)
  blocking collectives  9.12 us (9%)
  other arithmetic  2.43 us (2%)
    all_gather x1, waiting for transfers between devices, per_device(): summed = jnp.sum(lax.all_gather(partial_terms, 'section'), axis=0) * scale  53.3 us
    dot_general x1, matrix products, per_device(): outer = jnp.dot(row_block.T, col_block, precision=lax.Precision.HIGHEST)  11.3 us
    all_gather x1, blocking collectives, per_device(): features = lax.all_gather(summed, 'dp', axis=0, tiled=True)  9.12 us
    dot_general x1, matrix products, per_device(): jnp.einsum('pkd,etd->pekt', layer_out, layer_grad, preferred_element_type...  4.78 us
    dot_general x1, matrix products, per_device(): jnp.einsum('pekt,petm->ekm', low_out, low_in, preferred_element_type=jnp....  3.63 us
    reduce_sum x1, other arithmetic, per_device(): summed = jnp.sum(lax.all_gather(partial_terms, 'section'), axis=0) * scale  2.4 us
  transfers between devices with their start and end apart: 1, of which 1 were waited for; matrix products, arithmetic and copies ran while one was open for 0% of the time, Pallas kernels for 0%

profile of v1, /device:TPU:0, one launch (start us, length us, event | category | flops | bytes accessed | tf_op | source)
XLA Modules:
  0.0 98.8 jit_solution(15637832693083162753)
XLA Ops:
  6.5 0.0 copy-start
  6.5 0.0 all-gather.2.cloned.1.call-start
  6.5 4.8 %fusion.13 = bf16[2,8,64,64]{3,2,0,1:T(8,128)(2,1)S(1)} fusion(bf16[1,8,64,4096]{3,2,1,0:T(8,128)(2,1)} %param.6, bf16[1,2,64,4096]{3,2,1,0:T(8,128)(2,1)} %param.8), kind=kOutput, calls=%fused_computation.8 | convolution fusion | flops 536936448 | bytes 5373952 | tf_op jit(solution)/shard_map/pkd,etd->pekt/dot_general | solution.py:19
  11.3 0.0 copy-done
  11.3 3.6 %convolution_bitcast_fusion = f32[8,64,128]{2,1,0:T(8,128)S(1)} fusion(bf16[2,8,64,64]{3,2,0,1:T(8,128)(2,1)S(1)} %fusion.13, bf16[1,8,64,4096]{3,2,1,0:T(8,128)(2,1)} %param.5, bf16[1,2,4096,128]{3,2,1,0:T(8,128)(2,1)S(1)} %copy-done), kind=kOutput, calls=%fused_computation.9 | convolution fusion | flops 1090650112 | bytes 6684672 | tf_op jit(solution)/shard_map/pekt,petm->ekm/dot_general | solution.py:22
  15.0 0.8 all_gather_reshape.3
  15.7 0.0 all-gather.2.cloned.1.call-update
  15.8 53.3 %all-gather.2.cloned.1.call-done = f32[16,8,8192]{2,1,0:T(8,128)} async-done(((f32[1,8,8192]{2,1,0:T(8,128)}), f32[16,8,8192]{2,1,0:T(8,128)}) %all-gather.2.cloned.1.call-update) | async-done | bytes 4194320 | tf_op jit(solution)/shard_map/all_gather | solution.py:35
  69.0 2.4 %reduce_sum.9 = f32[8,8192]{1,0:T(8,128)S(1)} reduce(f32[16,8,8192]{2,1,0:T(8,128)} %all-gather.2.cloned.1.call-done, f32[]{:T(128)} %constant.9.clone.1), dimensions={0}, to_apply=%region_0.0 | reduce | flops 983040 | bytes 4456452 | tf_op jit(solution)/shard_map/reduce_sum | solution.py:35
  71.5 9.1 %all_gather.7 = f32[16,8192]{1,0:T(8,128)S(1)} all-gather(f32[8,8192]{1,0:T(8,128)S(1)} %broadcast_multiply_fusion), channel_id=1, replica_groups=mesh['section'=16,'dp'=2] {'dp'}, dimensions={0}, use_global_device_ids=true | all-gather | bytes 786432 | tf_op jit(solution)/shard_map/all_gather | solution.py:36
  80.6 11.3 %multiply_add_fusion = f32[512,4096]{1,0:T(8,128)} fusion(f32[512,4096]{1,0:T(8,128)} %param.9, f32[16,8192]{1,0:T(8,128)S(1)} %all_gather.7, s32[]{:T(128)S(6)} %select_n.7, s32[]{:T(128)S(6)} %select_n.6), kind=kOutput, calls=%fused_computation | convolution fusion | flops 406847488 | bytes 17072136 | tf_op jit(solution)/shard_map/dot_general | solution.py:39
  (1 shorter events, 0.0 us)
Async XLA Ops:
  6.5 4.8 %copy-start = (bf16[1,2,4096,128]{3,2,1,0:T(8,128)(2,1)S(1)}, bf16[1,2,4096,128]{3,2,1,0:T(8,128)(2,1)}, u32[]{:S(2)}) copy-start(bf16[1,2,4096,128]{3,2,1,0:T(8,128)(2,1)} %param.7) | copy-start | bytes 6291460
  6.5 62.5 %all-gather.2.cloned.1.call-start = ((), (), s32[]{:S(2)}) async-start(), calls=%async_computation | async-start | bytes 4456448 | tf_op jit(solution)/shard_map/all_gather | solution.py:35
Sparse Core Ops, SparseCore 0:
  15.9 53.0 all-gather.1
